TPU v7x, 512 devices: a whole 4x8x8 slice. The times are simulated.
512 devices in a mesh: blk: 8 (over y_lo, core), team: 64 (over y_hi, x, z).
Axes of the slice: x: 4, y: 8 (y_hi: 2, y_lo: 4; y = y_hi * 4 + y_lo), z: 8, core: 2. Of those that a mesh axis runs over, the one named last changes fastest.
Arguments:
- features: bfloat16 [65536, 256], P(('blk', 'team')), may hold values from -6 to 6
- weight: bfloat16 [256, 256], replicated, may hold values from -0.375 to 0.375
- bias: float32 [256], replicated, may hold values from -3 to 3
- cotangent: bfloat16 [65536, 256], P(('blk', 'team')), may hold values from -6 to 6
- adj_cols: int32 [64, 8, 8, 12], P('team', None, 'blk'), may hold values from 0 to 63, as said below
- adj_vals: bfloat16 [64, 8, 8, 12, 128, 128], P('team', None, 'blk'), as said below
Outputs:
- hidden: bfloat16 [65536, 256], P(('blk', 'team'))
- grad_input: bfloat16 [65536, 256], P(('blk', 'team'))
- grad_weight: float32 [256, 256], replicated
- grad_bias: float32 [256], replicated
Inputs may be any that keep to these rules, and one draw needn't show every extreme that they name: `adj_cols`: for every node panel and column group the 12 entries are distinct. Block (i, j) of A is listed exactly when block (j, i) is, every column panel is listed by exactly 12 row panels of each column group, and A is symmetric. `adj_vals`: the block listed for panels (i, j) is the transpose of the block listed for (j, i), so A is symmetric.
All inputs are finite; a program needn't handle non-finite values.
Results may differ from a plain program's by a relative error of at most 0.0075.
Values may be sent and summed in bfloat16 or wider, within the bound.
No kernel may reach another device: no remote copies, remote signals or barrier semaphores. Data moves between devices by JAX's collectives and lax.ppermute only.
A program may use at most 64 MiB of HBM per device.

v0:
```python
import jax
import jax.numpy as jnp
from jax import lax
from jax.sharding import Mesh
from jax.sharding import PartitionSpec as P

BLK_AXES = ("y_lo", "core")
TEAM_AXES = ("y_hi", "x", "z")
PLANE = ("x", "z")
ALL_AXES = BLK_AXES + TEAM_AXES


def fine_mesh(mesh):
    blk = mesh.shape["blk"]
    team = mesh.shape["team"]
    sizes = (blk // 2, 2, 2, 4, team // 8)
    return Mesh(mesh.devices.reshape(sizes), ALL_AXES)


def gather_team(rows):
    other = lax.ppermute(rows, "y_hi", perm=[(0, 1), (1, 0)])
    pair = jnp.stack([rows, other], axis=0)
    full = lax.all_gather(pair, PLANE, axis=0, tiled=True)
    return full.reshape(-1, rows.shape[1])


def member_slots(members, plane_size):
    my_hi = lax.axis_index("y_hi")
    return members % plane_size * 2 + (members // plane_size != my_hi).astype(jnp.int32)


def collect(panels, slots, adj_vals):
    block = adj_vals.shape[-1]
    width = panels.shape[1]
    stacked = panels.reshape(panels.shape[0] // block, block, width)
    picked = jnp.take(stacked, slots, axis=0)
    summed = jnp.einsum(
        "rkij,rkjf->rif", adj_vals[0, :, 0], picked, preferred_element_type=jnp.float32
    )
    return summed.reshape(-1, width)


def activation(value):
    return jax.nn.gelu(value, approximate=True)


def local(features, weight, bias, cotangent, adj_cols, adj_vals):
    plane_size = lax.psum(1, PLANE)
    slots = member_slots(adj_cols[0, :, 0, :], plane_size)
    product = jnp.dot(features, weight, preferred_element_type=jnp.float32).astype(jnp.bfloat16)
    gathered = gather_team(product)
    partial_rows = collect(gathered, slots, adj_vals)
    summed = lax.psum_scatter(partial_rows, BLK_AXES, scatter_dimension=0, tiled=True)
    pre = summed + bias[None, :]
    activated, pullback = jax.vjp(activation, pre)
    hidden = activated.astype(jnp.bfloat16)
    pulled = pullback(cotangent.astype(jnp.float32))[0].astype(jnp.bfloat16)
    pulled_group = gather_team(pulled)
    partial_back = collect(pulled_group, slots, adj_vals)
    spread = lax.psum_scatter(partial_back, BLK_AXES, scatter_dimension=0, tiled=True).astype(
        jnp.bfloat16
    )
    grad_input = jnp.dot(spread, weight.T, preferred_element_type=jnp.float32).astype(jnp.bfloat16)
    local_weight = lax.dot_general(
        features, spread, (((0,), (0,)), ((), ())), preferred_element_type=jnp.float32
    )
    local_bias = jnp.sum(pulled.astype(jnp.float32), axis=0)
    both = jnp.concatenate([local_weight, local_bias[None, :]], axis=0)
    both = lax.psum(both, PLANE)
    both = lax.psum(both, ("y_lo", "y_hi", "core"))
    grad_weight = both[:-1]
    grad_bias = both[-1]
    return (hidden, grad_input, grad_weight, grad_bias)


def solution(mesh):
    fine = fine_mesh(mesh)
    rows = P(ALL_AXES, None)
    return jax.shard_map(
        local,
        mesh=fine,
        in_specs=(
            rows,
            P(),
            P(),
            rows,
            P(TEAM_AXES, None, BLK_AXES, None),
            P(TEAM_AXES, None, BLK_AXES, None, None, None),
        ),
        out_specs=(rows, rows, P(), P()),
        check_vma=False,
    )
```

profile of v0, /device:TPU:1, one launch (start us, length us, event | category | flops | bytes accessed | tf_op | source)
XLA Modules:
  0.0 590.6 jit_solution(9726838023997011577)
XLA Ops:
  7.2 0.0 copy-start
  7.2 0.0 all-gather.3.cloned.1.call-start
  7.2 1.2 convolution_convert_fusion.1
  8.5 8.3 %collective-permute-start = (bf16[128,256]{1,0:T(8,128)(2,1)S(1)}, bf16[128,256]{1,0:T(8,128)(2,1)S(1)}, u32[]{:S(2)}, u32[]{:S(2)}) collective-permute-start(bf16[128,256]{1,0:T(8,128)(2,1)S(1)} %convolution_convert_fusion.1), channel_id=1, source_target_pairs={{0,32},{32,0},{1,33},{33,1},{2,34},{34,2},{3,35},{35,3},{4,36},{36... | collective-permute-start | bytes 196616 | tf_op jit(solution)/shard_map/ppermute | solution.py:21
  16.8 1.7 collective-permute-done
  18.5 0.7 pad_maximum_fusion.1
  19.1 0.0 all-gather.3.cloned.1.call-update
  19.2 0.0 reduce-scatter.3.cloned.1.call-start
  19.2 0.7 compare_and_fusion
  19.9 0.1 reshape.42
  20.0 91.1 %all-gather.3.cloned.1.call-done = bf16[64,128,256]{2,1,0:T(8,128)(2,1)} async-done(((bf16[2,128,256]{2,1,0:T(8,128)(2,1)}), bf16[64,128,256]{2,1,0:T(8,128)(2,1)}) %all-gather.3.cloned.1.call-update) | async-done | bytes 4194320 | tf_op jit(solution)/shard_map/all_gather | solution.py:23
  111.1 8.2 %gather_fusion = bf16[96,128,256]{2,1,0:T(8,128)(2,1)} fusion(bf16[64,128,256]{2,1,0:T(8,128)(2,1)} %all-gather.3.cloned.1.call-done, s32[1024]{0:T(1024)S(1)} %pad_clamp_fusion), kind=kCustom, calls=%fused_computation.clone | custom fusion | bytes 12583296 | tf_op jit(solution)/shard_map/jit(_take)/gather | solution.py:36
  119.3 0.0 copy-done
  119.3 0.0 copy-start.3
  119.3 0.0 copy-start.4
  119.3 5.2 fusion.2
  124.5 0.0 reduce-scatter.3.cloned.1.call-update
  124.5 0.0 all-gather.5.cloned.1.call-start
  124.6 38.0 %reduce-scatter.3.cloned.1.call-done = f32[128,256]{1,0:T(8,128)} async-done(((f32[1024,256]{1,0:T(8,128)}), f32[128,256]{1,0:T(8,128)}) %reduce-scatter.3.cloned.1.call-update) | async-done | bytes 131088 | tf_op jit(solution)/shard_map/reduce_scatter | solution.py:53
  162.5 0.0 copy-done.3
  162.5 0.0 copy-done.4
  162.5 1.6 convert_reduce_fusion
  164.2 5.5 collective-permute-start.1
  169.6 3.7 collective-permute-done.1
  173.3 0.7 pad_maximum_fusion.2
  174.0 0.0 all-gather.5.cloned.1.call-update
  174.0 0.0 reduce-scatter.5.cloned.1.call-start
  174.1 86.9 %all-gather.5.cloned.1.call-done = bf16[64,128,256]{2,1,0:T(8,128)(2,1)} async-done(((bf16[2,128,256]{2,1,0:T(8,128)(2,1)}), bf16[64,128,256]{2,1,0:T(8,128)(2,1)}) %all-gather.5.cloned.1.call-update) | async-done | bytes 4194320 | tf_op jit(solution)/shard_map/all_gather | solution.py:23
  260.9 8.2 %gather_fusion.1 = bf16[96,128,256]{2,1,0:T(8,128)(2,1)} fusion(bf16[64,128,256]{2,1,0:T(8,128)(2,1)} %all-gather.5.cloned.1.call-done, s32[1024]{0:T(1024)S(1)} %pad_clamp_fusion), kind=kCustom, calls=%fused_computation.1.clone | custom fusion | bytes 12583296 | tf_op jit(solution)/shard_map/jit(_take)/gather | solution.py:36
  269.1 0.0 copy-start.2
  269.1 0.0 copy-start.1
  269.1 5.2 fusion
  274.3 0.0 reduce-scatter.5.cloned.1.call-update
  274.3 0.0 all-reduce.3.cloned.1.call-start
  274.4 38.0 %reduce-scatter.5.cloned.1.call-done = f32[128,256]{1,0:T(8,128)} async-done(((f32[1024,256]{1,0:T(8,128)}), f32[128,256]{1,0:T(8,128)}) %reduce-scatter.5.cloned.1.call-update) | async-done | bytes 131088 | tf_op jit(solution)/shard_map/reduce_scatter | solution.py:60
  312.3 0.0 copy-done.2
  312.3 1.1 convolution_bitcast_fusion
  313.5 0.7 pad_maximum_fusion
  314.2 0.0 all-reduce.3.cloned.1.call-update
  314.2 0.0 all-reduce.5.cloned.1.call-start
  314.3 153.2 %all-reduce.3.cloned.1.call-done = f32[257,256]{1,0:T(8,128)} async-done(((f32[257,256]{1,0:T(8,128)}), f32[257,256]{1,0:T(8,128)}) %all-reduce.3.cloned.1.call-update) | async-done | bytes 263184 | tf_op jit(solution)/shard_map/psum | solution.py:69
  467.4 0.0 all-reduce.5.cloned.1.call-update
  467.5 0.0 copy-done.1
  467.5 1.7 convolution_convert_fusion
  469.2 111.6 %all-reduce.5.cloned.1.call-done = f32[257,256]{1,0:T(8,128)} async-done(((f32[257,256]{1,0:T(8,128)}), f32[257,256]{1,0:T(8,128)}) %all-reduce.5.cloned.1.call-update) | async-done | bytes 263184 | tf_op jit(solution)/shard_map/psum | solution.py:70
  580.8 1.3 slice.13
  582.1 1.7 slice.12
  (1 shorter events, 0.0 us)
Async XLA Ops:
  7.2 112.1 %copy-start = (bf16[1,8,1,12,128,128]{5,4,3,2,1,0:T(8,128)(2,1)S(1)}, bf16[1,8,1,12,128,128]{5,4,3,2,1,0:T(8,128)(2,1)}, u32[]{:S(2)}) copy-start(bf16[1,8,1,12,128,128]{5,4,3,2,1,0:T(8,128)(2,1)} %param.13) | copy-start | bytes 9437188
  7.2 103.9 %all-gather.3.cloned.1.call-start = ((), (), s32[]{:S(2)}) async-start(), calls=%async_computation.2 | async-start | bytes 4325376 | tf_op jit(solution)/shard_map/all_gather | solution.py:23
  8.5 10.0 %collective-permute-start = (bf16[128,256]{1,0:T(8,128)(2,1)S(1)}, bf16[128,256]{1,0:T(8,128)(2,1)S(1)}, u32[]{:S(2)}, u32[]{:S(2)}) collective-permute-start(bf16[128,256]{1,0:T(8,128)(2,1)S(1)} %convolution_convert_fusion.1), channel_id=1, source_target_pairs={{0,32},{32,0},{1,33},{33,1},{2,34},{34,2},{3,35},{35,3},{4,36},{36... | collective-permute-start | bytes 196616 | tf_op jit(solution)/shard_map/ppermute | solution.py:21
  19.2 143.4 %reduce-scatter.3.cloned.1.call-start = ((), (), s32[]{:S(2)}) async-start(), calls=%async_computation.3 | async-start | bytes 1179648 | tf_op jit(solution)/shard_map/reduce_scatter | solution.py:53
  119.3 43.2 %copy-start.3 = (bf16[128,256]{1,0:T(8,128)(2,1)S(1)}, bf16[128,256]{1,0:T(8,128)(2,1)}, u32[]{:S(2)}) copy-start(bf16[128,256]{1,0:T(8,128)(2,1)} %param.11) | copy-start | bytes 196612
  119.3 43.2 %copy-start.4 = (f32[256]{0:T(256)S(1)}, f32[256]{0:T(256)}, u32[]{:S(2)}) copy-start(f32[256]{0:T(256)} %param.10) | copy-start | bytes 3076
  124.5 136.4 %all-gather.5.cloned.1.call-start = ((), (), s32[]{:S(2)}) async-start(), calls=%async_computation.4 | async-start | bytes 4325376 | tf_op jit(solution)/shard_map/all_gather | solution.py:23
  164.2 9.1 %collective-permute-start.1 = (bf16[128,256]{1,0:T(8,128)(2,1)S(1)}, bf16[128,256]{1,0:T(8,128)(2,1)S(1)}, u32[]{:S(2)}, u32[]{:S(2)}) collective-permute-start(bf16[128,256]{1,0:T(8,128)(2,1)S(1)} %get-tuple-element.6), channel_id=1, source_target_pairs={{0,32},{32,0},{1,33},{33,1},{2,34},{34,2},{3,35},{35,3},{4,36},{36... | collective-permute-start | bytes 196616 | tf_op jit(solution)/shard_map/ppermute | solution.py:21
  174.0 138.3 %reduce-scatter.5.cloned.1.call-start = ((), (), s32[]{:S(2)}) async-start(), calls=%async_computation.5 | async-start | bytes 1179648 | tf_op jit(solution)/shard_map/reduce_scatter | solution.py:60
  269.1 43.2 %copy-start.2 = (bf16[128,256]{1,0:T(8,128)(2,1)S(1)}, bf16[128,256]{1,0:T(8,128)(2,1)}, u32[]{:S(2)}) copy-start(bf16[128,256]{1,0:T(8,128)(2,1)} %param.8) | copy-start | bytes 196612
  269.1 198.3 %copy-start.1 = (bf16[256,256]{1,0:T(8,128)(2,1)S(1)}, bf16[256,256]{1,0:T(8,128)(2,1)}, u32[]{:S(2)}) copy-start(bf16[256,256]{1,0:T(8,128)(2,1)} %param.9) | copy-start | bytes 393220
  274.3 193.1 %all-reduce.3.cloned.1.call-start = ((), (), s32[]{:S(2)}) async-start(), calls=%async_computation.6 | async-start | bytes 540672 | tf_op jit(solution)/shard_map/psum | solution.py:69
  314.2 266.6 %all-reduce.5.cloned.1.call-start = ((), (), s32[]{:S(2)}) async-start(), calls=%async_computation.7 | async-start | bytes 540672 | tf_op jit(solution)/shard_map/psum | solution.py:70
Sparse Core Ops, SparseCore 0:
  19.3 91.7 all-gather.2
  124.6 37.8 reduce-scatter.2
  174.1 86.7 all-gather.4
  274.5 37.8 reduce-scatter.4
  315.6 151.7 all-reduce.2
  469.6 111.1 all-reduce.4
where the time goes:
time: 591 us
  waiting for transfers between devices  524 us (89%)
  local copies, waits for them, and re-layouts  19.4 us (3%)
  matrix products  14.5 us (2%)
  between operations  14.2 us (2%)
  starting transfers between devices  14 us (2%)
    all_gather x2, waiting for transfers between devices, gather_team(): full = lax.all_gather(pair, PLANE, axis=0, tiled=True)  178 us
    psum x1, waiting for transfers between devices, local(): both = lax.psum(both, PLANE)  153 us
    psum x1, waiting for transfers between devices, local(): both = lax.psum(both, ('y_lo', 'y_hi', 'core'))  112 us
    reduce_scatter x1, waiting for transfers between devices, local(): lax.psum_scatter(partial_back, BLK_AXES, scatter_dimension=0, tiled=True)  38 us
    reduce_scatter x1, waiting for transfers between devices, local(): lax.psum_scatter(partial_rows, BLK_AXES, scatter_dimension=0, tiled=True)  38 us
    gather x2, local copies, waits for them, and re-layouts, collect(): picked = jnp.take(stacked, slots, axis=0)  16.4 us
    ppermute x2, starting transfers between devices, gather_team(): other = lax.ppermute(rows, 'y_hi', perm=[(0, 1), (1, 0)])  13.7 us
  transfers between devices with their start and end apart: 8, of which 8 were waited for; matrix products, arithmetic and copies ran while one was open for 0% of the time, Pallas kernels for 0%

commit v1 on v0

--- a/solution.py
+++ b/solution.py
@@ -66,7 +66,7 @@
     )
     local_bias = jnp.sum(pulled.astype(jnp.float32), axis=0)
     both = jnp.concatenate([local_weight, local_bias[None, :]], axis=0)
-    both = lax.psum(both, PLANE)
+    both = jnp.sum(lax.all_gather(both, PLANE), axis=0)
     both = lax.psum(both, ("y_lo", "y_hi", "core"))
     grad_weight = both[:-1]
     grad_bias = both[-1]

time: 591 us -> 544 us (0.920)
  waiting for transfers between devices: 524 us -> 473 us
    psum x1 -> x0, waiting for transfers between devices: 153 us -> none  [local(): both = lax.psum(both, PLANE)]
    all_gather x0 -> x1, waiting for transfers between devices: none -> 107 us  [local(): both = jnp.sum(lax.all_gather(both, PLANE), axis=0)]
where the time goes in v1:
time: 544 us
  waiting for transfers between devices  473 us (87%)
  local copies, waits for them, and re-layouts  19.4 us (4%)
  starting transfers between devices  14.3 us (3%)
  between operations  14.2 us (3%)
  matrix products  13.7 us (3%)
  other arithmetic  9.19 us (2%)
    all_gather x2, waiting for transfers between devices, gather_team(): full = lax.all_gather(pair, PLANE, axis=0, tiled=True)  178 us
    all_gather x1, waiting for transfers between devices, local(): both = jnp.sum(lax.all_gather(both, PLANE), axis=0)  107 us
    psum x1, waiting for transfers between devices, local(): both = lax.psum(both, ('y_lo', 'y_hi', 'core'))  107 us
    reduce_scatter x1, waiting for transfers between devices, local(): lax.psum_scatter(partial_rows, BLK_AXES, scatter_dimension=0, tiled=True)  37.9 us
    reduce_scatter x1, waiting for transfers between devices, local(): lax.psum_scatter(partial_back, BLK_AXES, scatter_dimension=0, tiled=True)  37.9 us
    gather x2, local copies, waits for them, and re-layouts, collect(): picked = jnp.take(stacked, slots, axis=0)  16.4 us
    ppermute x2, starting transfers between devices, gather_team(): other = lax.ppermute(rows, 'y_hi', perm=[(0, 1), (1, 0)])  14.1 us
  transfers between devices with their start and end apart: 8, of which 8 were waited for; matrix products, arithmetic and copies ran while one was open for 0% of the time, Pallas kernels for 0%

profile of v1, /device:TPU:1, one launch (start us, length us, event | category | flops | bytes accessed | tf_op | source)
XLA Modules:
  0.0 543.8 jit_solution(10497180695089417400)
XLA Ops:
  7.2 0.0 copy-start
  7.2 0.0 all-gather.6.cloned.1.call-start
  7.2 1.2 convolution_convert_fusion.1
  8.5 8.3 %collective-permute-start = (bf16[128,256]{1,0:T(8,128)(2,1)S(1)}, bf16[128,256]{1,0:T(8,128)(2,1)S(1)}, u32[]{:S(2)}, u32[]{:S(2)}) collective-permute-start(bf16[128,256]{1,0:T(8,128)(2,1)S(1)} %convolution_convert_fusion.1), channel_id=1, source_target_pairs={{0,32},{32,0},{1,33},{33,1},{2,34},{34,2},{3,35},{35,3},{4,36},{36... | collective-permute-start | bytes 196616 | tf_op jit(solution)/shard_map/ppermute | solution.py:21
  16.8 1.7 collective-permute-done
  18.5 0.7 pad_maximum_fusion
  19.1 0.0 all-gather.6.cloned.1.call-update
  19.2 0.0 reduce-scatter.3.cloned.1.call-start
  19.2 0.7 compare_and_fusion
  19.9 0.1 reshape.46
  20.0 91.1 %all-gather.6.cloned.1.call-done = bf16[64,128,256]{2,1,0:T(8,128)(2,1)} async-done(((bf16[2,128,256]{2,1,0:T(8,128)(2,1)}), bf16[64,128,256]{2,1,0:T(8,128)(2,1)}) %all-gather.6.cloned.1.call-update) | async-done | bytes 4194320 | tf_op jit(solution)/shard_map/all_gather | solution.py:23
  111.1 8.2 %gather_fusion = bf16[96,128,256]{2,1,0:T(8,128)(2,1)} fusion(bf16[64,128,256]{2,1,0:T(8,128)(2,1)} %all-gather.6.cloned.1.call-done, s32[1024]{0:T(1024)S(1)} %pad_clamp_fusion), kind=kCustom, calls=%fused_computation.clone | custom fusion | bytes 12583296 | tf_op jit(solution)/shard_map/jit(_take)/gather | solution.py:36
  119.3 0.0 copy-done
  119.3 0.0 copy-start.4
  119.3 0.0 copy-start.5
  119.3 5.2 fusion.2
  124.5 0.0 reduce-scatter.3.cloned.1.call-update
  124.5 0.0 all-gather.8.cloned.1.call-start
  124.6 37.9 %reduce-scatter.3.cloned.1.call-done = f32[128,256]{1,0:T(8,128)} async-done(((f32[1024,256]{1,0:T(8,128)}), f32[128,256]{1,0:T(8,128)}) %reduce-scatter.3.cloned.1.call-update) | async-done | bytes 131088 | tf_op jit(solution)/shard_map/reduce_scatter | solution.py:53
  162.5 0.0 copy-done.4
  162.5 0.0 copy-done.5
  162.5 1.6 convert_reduce_fusion
  164.1 5.8 %collective-permute-start.1 = (bf16[128,256]{1,0:T(8,128)(2,1)S(1)}, bf16[128,256]{1,0:T(8,128)(2,1)S(1)}, u32[]{:S(2)}, u32[]{:S(2)}) collective-permute-start(bf16[128,256]{1,0:T(8,128)(2,1)S(1)} %get-tuple-element.6), channel_id=1, source_target_pairs={{0,32},{32,0},{1,33},{33,1},{2,34},{34,2},{3,35},{35,3},{4,36},{36... | collective-permute-start | bytes 196616 | tf_op jit(solution)/shard_map/ppermute | solution.py:21
  170.0 3.4 collective-permute-done.1
  173.4 0.7 pad_maximum_fusion.1
  174.1 0.0 all-gather.8.cloned.1.call-update
  174.1 0.0 reduce-scatter.5.cloned.1.call-start
  174.1 86.8 %all-gather.8.cloned.1.call-done = bf16[64,128,256]{2,1,0:T(8,128)(2,1)} async-done(((bf16[2,128,256]{2,1,0:T(8,128)(2,1)}), bf16[64,128,256]{2,1,0:T(8,128)(2,1)}) %all-gather.8.cloned.1.call-update) | async-done | bytes 4194320 | tf_op jit(solution)/shard_map/all_gather | solution.py:23
  260.9 8.2 %gather_fusion.1 = bf16[96,128,256]{2,1,0:T(8,128)(2,1)} fusion(bf16[64,128,256]{2,1,0:T(8,128)(2,1)} %all-gather.8.cloned.1.call-done, s32[1024]{0:T(1024)S(1)} %pad_clamp_fusion), kind=kCustom, calls=%fused_computation.1.clone | custom fusion | bytes 12583296 | tf_op jit(solution)/shard_map/jit(_take)/gather | solution.py:36
  269.1 0.0 copy-start.3
  269.1 5.2 fusion
  274.3 0.0 copy-start.2
  274.3 0.0 reduce-scatter.5.cloned.1.call-update
  274.3 0.0 all-gather.10.cloned.1.call-start
  274.4 37.9 %reduce-scatter.5.cloned.1.call-done = f32[128,256]{1,0:T(8,128)} async-done(((f32[1024,256]{1,0:T(8,128)}), f32[128,256]{1,0:T(8,128)}) %reduce-scatter.5.cloned.1.call-update) | async-done | bytes 131088 | tf_op jit(solution)/shard_map/reduce_scatter | solution.py:60
  312.3 0.0 copy-done.3
  312.3 0.0 copy-start.1
  312.3 1.2 convolution_bitcast_fusion
  313.5 0.7 maximum_bitcast_fusion
  314.2 0.0 all-gather.10.cloned.1.call-update
  314.2 0.0 all-reduce.2.cloned.1.call-start
  314.3 107.4 %all-gather.10.cloned.1.call-done = f32[32,257,256]{2,1,0:T(8,128)} async-done(((f32[1,257,256]{2,1,0:T(8,128)}), f32[32,257,256]{2,1,0:T(8,128)}) %all-gather.10.cloned.1.call-update) | async-done | bytes 8421392 | tf_op jit(solution)/shard_map/all_gather | solution.py:69
  421.7 4.7 reduce_sum.19
  426.5 0.0 all-reduce.2.cloned.1.call-update
  426.5 0.0 copy-done.2
  426.5 0.0 copy-done.1
  426.5 0.8 convolution_convert_fusion
  427.4 106.6 %all-reduce.2.cloned.1.call-done = f32[257,256]{1,0:T(8,128)} async-done(((f32[257,256]{1,0:T(8,128)}), f32[257,256]{1,0:T(8,128)}) %all-reduce.2.cloned.1.call-update) | async-done | bytes 263184 | tf_op jit(solution)/shard_map/psum | solution.py:70
  534.0 1.3 slice.13
  535.3 1.7 slice.12
  (1 shorter events, 0.0 us)
Async XLA Ops:
  7.2 112.1 %copy-start = (bf16[1,8,1,12,128,128]{5,4,3,2,1,0:T(8,128)(2,1)S(1)}, bf16[1,8,1,12,128,128]{5,4,3,2,1,0:T(8,128)(2,1)}, u32[]{:S(2)}) copy-start(bf16[1,8,1,12,128,128]{5,4,3,2,1,0:T(8,128)(2,1)} %param.13) | copy-start | bytes 9437188
  7.2 103.9 %all-gather.6.cloned.1.call-start = ((), (), s32[]{:S(2)}) async-start(), calls=%async_computation.2 | async-start | bytes 4325376 | tf_op jit(solution)/shard_map/all_gather | solution.py:23
  8.5 10.0 %collective-permute-start = (bf16[128,256]{1,0:T(8,128)(2,1)S(1)}, bf16[128,256]{1,0:T(8,128)(2,1)S(1)}, u32[]{:S(2)}, u32[]{:S(2)}) collective-permute-start(bf16[128,256]{1,0:T(8,128)(2,1)S(1)} %convolution_convert_fusion.1), channel_id=1, source_target_pairs={{0,32},{32,0},{1,33},{33,1},{2,34},{34,2},{3,35},{35,3},{4,36},{36... | collective-permute-start | bytes 196616 | tf_op jit(solution)/shard_map/ppermute | solution.py:21
  19.2 143.3 %reduce-scatter.3.cloned.1.call-start = ((), (), s32[]{:S(2)}) async-start(), calls=%async_computation.3 | async-start | bytes 1179648 | tf_op jit(solution)/shard_map/reduce_scatter | solution.py:53
  119.3 43.2 %copy-start.4 = (bf16[128,256]{1,0:T(8,128)(2,1)S(1)}, bf16[128,256]{1,0:T(8,128)(2,1)}, u32[]{:S(2)}) copy-start(bf16[128,256]{1,0:T(8,128)(2,1)} %param.11) | copy-start | bytes 196612
  119.3 43.2 %copy-start.5 = (f32[256]{0:T(256)S(1)}, f32[256]{0:T(256)}, u32[]{:S(2)}) copy-start(f32[256]{0:T(256)} %param.10) | copy-start | bytes 3076
  124.5 136.4 %all-gather.8.cloned.1.call-start = ((), (), s32[]{:S(2)}) async-start(), calls=%async_computation.4 | async-start | bytes 4325376 | tf_op jit(solution)/shard_map/all_gather | solution.py:23
  164.1 9.3 %collective-permute-start.1 = (bf16[128,256]{1,0:T(8,128)(2,1)S(1)}, bf16[128,256]{1,0:T(8,128)(2,1)S(1)}, u32[]{:S(2)}, u32[]{:S(2)}) collective-permute-start(bf16[128,256]{1,0:T(8,128)(2,1)S(1)} %get-tuple-element.6), channel_id=1, source_target_pairs={{0,32},{32,0},{1,33},{33,1},{2,34},{34,2},{3,35},{35,3},{4,36},{36... | collective-permute-start | bytes 196616 | tf_op jit(solution)/shard_map/ppermute | solution.py:21
  174.1 138.2 %reduce-scatter.5.cloned.1.call-start = ((), (), s32[]{:S(2)}) async-start(), calls=%async_computation.5 | async-start | bytes 1179648 | tf_op jit(solution)/shard_map/reduce_scatter | solution.py:60
  269.1 43.2 %copy-start.3 = (bf16[128,256]{1,0:T(8,128)(2,1)S(1)}, bf16[128,256]{1,0:T(8,128)(2,1)}, u32[]{:S(2)}) copy-start(bf16[128,256]{1,0:T(8,128)(2,1)} %param.8) | copy-start | bytes 196612
  274.3 152.2 %copy-start.2 = (bf16[256,256]{1,0:T(8,128)(2,1)S(1)}, bf16[256,256]{1,0:T(8,128)(2,1)}, u32[]{:S(2)}) copy-start(bf16[256,256]{1,0:T(8,128)(2,1)} %param.9) | copy-start | bytes 393220
  274.3 147.4 %all-gather.10.cloned.1.call-start = ((), (), s32[]{:S(2)}) async-start(), calls=%async_computation.7 | async-start | bytes 8921088 | tf_op jit(solution)/shard_map/all_gather | solution.py:69
  312.3 114.2 %copy-start.1 = (f32[128,256]{1,0:T(8,128)S(1)}, f32[128,256]{1,0:T(8,128)}, u32[]{:S(2)}) copy-start(f32[128,256]{1,0:T(8,128)} %reduce-scatter.5.cloned.1.call-done) | copy-start | bytes 393220
  314.2 219.8 %all-reduce.2.cloned.1.call-start = ((), (), s32[]{:S(2)}) async-start(), calls=%async_computation.6 | async-start | bytes 540672 | tf_op jit(solution)/shard_map/psum | solution.py:70
Sparse Core Ops, SparseCore 0:
  19.3 91.7 all-gather.5
  124.7 37.7 reduce-scatter.2
  174.2 86.6 all-gather.7
  274.4 37.7 reduce-scatter.4
  315.3 106.4 all-gather.9
  426.6 107.3 all-reduce.1
